TPU v7x, 512 devices: a whole 4x8x8 slice. The times are simulated.
512 devices in a mesh: expert: 16 (over z, core), tensor: 32 (over x, y).
Axes of the slice: x: 4, y: 8, z: 8, core: 2. Of those that a mesh axis runs over, the one named last changes fastest.
Arguments:
- tokens: bfloat16 [2048, 5120], P('expert', 'tensor'), may hold values from -6 to 6
- routes: int32 [2048, 6], P('expert'), may hold values from 0 to 15, all different within a row; in each aligned block of 128 rows (0 to 127, 128 to 255, ...) at most 64 rows name the same one
- gates: float32 [2048, 6], P('expert'), may hold values from 0.05 to 0.35
- w_gate: bfloat16 [16, 1536, 5120], P('expert', 'tensor'), may hold values from -0.078125 to 0.078125
- w_up: bfloat16 [16, 1536, 5120], P('expert', 'tensor'), may hold values from -0.078125 to 0.078125
- w_down: bfloat16 [16, 1536, 5120], P('expert', None, 'tensor'), may hold values from -0.15625 to 0.15625
- shared_gate: bfloat16 [1536, 5120], P('tensor'), may hold values from -0.078125 to 0.078125
- shared_up: bfloat16 [1536, 5120], P('tensor'), may hold values from -0.078125 to 0.078125
- shared_down: bfloat16 [1536, 5120], P(None, 'tensor'), may hold values from -0.15625 to 0.15625
- vocab: bfloat16 [65536, 5120], P(('expert', 'tensor'))
- targets: int32 [64], replicated, may hold values from 0 to 65535
Outputs:
- layer_out: bfloat16 [2048, 5120], P('expert', 'tensor')
- loglik: float32 [64], replicated
Inputs may be any that keep to these rules, and one draw needn't show every extreme that they name: `routes`: the tokens of one group name one expert at most 64 times; in every draw some group names some expert exactly 64 times.
All inputs are finite; a program needn't handle non-finite values.
Results may differ from a plain program's by a relative error of at most 0.0041.
Values may be sent and summed in bfloat16 or wider, within the bound.
No kernel may reach another device: no remote copies, remote signals or barrier semaphores. Data moves between devices by JAX's collectives and lax.ppermute only.
A program may use at most 64 MiB of HBM per device.

v0:
```python
import jax
import jax.numpy as jnp
from jax import lax
from jax.sharding import PartitionSpec as P

EXPERTS = 16
SCORE_E = 4


def slot_tables(routes, gates, capacity):
    picks = (routes[:, :, None] == jnp.arange(EXPERTS, dtype=jnp.int32)[None, None, :]).astype(
        jnp.int32
    )
    per_token = jnp.sum(picks, axis=1)
    earlier = jnp.cumsum(per_token, axis=0) - per_token
    slots = jnp.sum(picks * earlier[:, None, :], axis=2)
    places = (slots[:, :, None] == jnp.arange(capacity, dtype=jnp.int32)[None, None, :]).astype(
        jnp.float32
    )
    picked = picks.astype(jnp.float32)
    select = jnp.einsum("ikr,iks->rsi", picked, places, precision=lax.Precision.HIGHEST)
    weigh = jnp.einsum("ikr,iks,ik->rsi", picked, places, gates, precision=lax.Precision.HIGHEST)
    return (select.astype(jnp.bfloat16), weigh)


def contract_last(left, right):
    return lax.dot_general(
        left, right, (((1,), (1,)), ((), ())), preferred_element_type=jnp.float32
    )


def shards(
    tokens, routes, gates, w_gate, w_up, w_down, shared_gate, shared_up, shared_down, vocab, targets
):
    tok_rows = tokens.shape[0]
    capacity = tok_rows // 2
    groups = lax.axis_size("expert")
    lanes = lax.axis_size("tensor")
    exp_dev = w_gate.shape[0]
    width = w_gate.shape[1]
    out_width = w_down.shape[2]
    select, weigh = slot_tables(routes, gates, capacity)
    outgoing = jnp.einsum("rsi,id->rsd", select, tokens, preferred_element_type=jnp.float32).astype(
        jnp.bfloat16
    )
    arrived = lax.all_to_all(outgoing, "expert", split_axis=0, concat_axis=1, tiled=True)
    slot_count = arrived.shape[1]
    flat_rows = arrived.reshape(exp_dev * slot_count, arrived.shape[2])
    pieces = (
        lax.all_gather(flat_rows, "tensor", axis=1, tiled=True),
        lax.all_gather(tokens, "tensor", axis=1, tiled=True),
    )
    span = pieces[0].shape[1]
    rows = pieces[0].reshape(exp_dev, slot_count, span)
    gate_acc = jnp.einsum("erw,efw->erf", rows, w_gate, preferred_element_type=jnp.float32)
    up_acc = jnp.einsum("erw,efw->erf", rows, w_up, preferred_element_type=jnp.float32)
    shared_gate_acc = contract_last(pieces[1], shared_gate)
    shared_up_acc = contract_last(pieces[1], shared_up)
    hidden_routed = (jax.nn.silu(gate_acc) * up_acc).astype(jnp.bfloat16)
    hidden_shared = (jax.nn.silu(shared_gate_acc) * shared_up_acc).astype(jnp.bfloat16)
    flat_hidden = hidden_routed.reshape(exp_dev * slot_count, width)
    pieces = (
        lax.all_gather(flat_hidden, "tensor", axis=1, tiled=True),
        lax.all_gather(hidden_shared, "tensor", axis=1, tiled=True),
    )
    span = pieces[0].shape[1]
    rows = pieces[0].reshape(exp_dev, slot_count, span)
    routed_out = jnp.einsum("erw,ewd->erd", rows, w_down, preferred_element_type=jnp.float32)
    shared_out = jnp.dot(pieces[1], shared_down, preferred_element_type=jnp.float32)
    returned = lax.all_to_all(
        routed_out.astype(jnp.bfloat16), "expert", split_axis=1, concat_axis=0, tiled=True
    )
    routed = jnp.einsum(
        "rsi,rsd->id", weigh, returned.astype(jnp.float32), precision=lax.Precision.HIGHEST
    )
    layer_out = (tokens.astype(jnp.float32) + shared_out + routed).astype(jnp.bfloat16)
    scored = layer_out[tok_rows - SCORE_E :].reshape(1, SCORE_E * out_width)
    collected = lax.all_gather(scored, ("expert", "tensor"), axis=0, tiled=True)
    full_rows = (
        collected.reshape(groups, lanes, SCORE_E, out_width)
        .transpose(0, 2, 1, 3)
        .reshape(groups * SCORE_E, lanes * out_width)
    )
    logits = contract_last(full_rows, vocab)
    exp_sums = jnp.sum(jnp.exp(logits), axis=1)
    offset = (lax.axis_index("expert") * lanes + lax.axis_index("tensor")) * vocab.shape[0]
    columns = offset + jnp.arange(vocab.shape[0], dtype=jnp.int32)
    target_part = jnp.sum(jnp.where(targets[:, None] == columns[None, :], logits, 0.0), axis=1)
    totals, target_logit = lax.psum((exp_sums, target_part), ("expert", "tensor"))
    loglik = target_logit - jnp.log(totals)
    return (layer_out, loglik)


def solution(mesh):
    placed = (
        P("expert", "tensor"),
        P("expert", None),
        P("expert", None),
        P("expert", "tensor", None),
        P("expert", "tensor", None),
        P("expert", None, "tensor"),
        P("tensor", None),
        P("tensor", None),
        P(None, "tensor"),
        P(("expert", "tensor"), None),
        P(),
    )
    return jax.shard_map(
        shards, mesh=mesh, in_specs=placed, out_specs=(P("expert", "tensor"), P()), check_vma=False
    )
```

profile of v0, /device:TPU:1, one launch (start us, length us, event | category | flops | bytes accessed | tf_op | source)
XLA Modules:
  0.0 622.9 jit_solution(7036797286087049021)
XLA Ops:
  7.2 0.9 copy.21
  8.6 2.4 select_reduce_fusion
  11.0 1.2 fusion
  12.6 29.1 %all_to_all.21 = bf16[16,64,160]{2,1,0:T(8,128)(2,1)S(1)} all-to-all(bf16[16,64,160]{2,1,0:T(8,128)(2,1)S(1)} %convolution_convert_fusion.1), channel_id=1, replica_groups=mesh['expert'=16,'tensor'=32] {'expert'}, dimensions={0} | all-to-all | bytes 655360 | tf_op jit(solution)/shard_map/all_to_all | solution.py:46
  41.7 0.9 copy.24
  42.7 110.4 %all-gather.7.cloned.1.call-done = bf16[1024,5120]{0,1:T(8,128)(2,1)} async-done(((bf16[1024,160]{0,1:T(8,128)(2,1)}), bf16[1024,5120]{0,1:T(8,128)(2,1)}) %all-gather.7.cloned.1.call-update) | async-done | bytes 10485776 | tf_op jit(solution)/shard_map/all_gather | solution.py:50
  153.1 6.1 fusion.11
  159.2 0.9 copy-done.1
  160.0 2.6 fusion.2
  162.9 0.5 all-gather.5.cloned.1.call-update
  163.6 2.7 convolution_bitcast_fusion
  166.3 76.0 %all-gather.9.cloned.1.call-done = bf16[1024,1536]{0,1:T(8,128)(2,1)} async-done(((bf16[1024,48]{0,1:T(8,128)(2,1)}), bf16[1024,1536]{0,1:T(8,128)(2,1)}) %all-gather.9.cloned.1.call-update) | async-done | bytes 3145744 | tf_op jit(solution)/shard_map/all_gather | solution.py:63
  242.3 2.6 fusion.1
  244.9 0.8 copy.25
  245.8 0.5 broadcast.28
  246.3 4.0 reduce.1
  250.3 1.5 reshape.84
  251.8 11.8 %all-to-all-start.1 = ((bf16[16,2,5120]{2,1,0:T(2,128)(2,1)}), bf16[16,2,5120]{2,1,0:T(2,128)(2,1)S(1)}, u32[]{:S(2)}, u32[]{:S(2)}) async-start(bf16[16,2,5120]{2,1,0:T(2,128)(2,1)} %reshape.84), calls=%async_computation.1 | async-start | bytes 655360 | tf_op jit(solution)/shard_map/all_to_all | solution.py:70
  263.6 60.0 %all-gather.5.cloned.1.call-done = bf16[128,5120]{0,1:T(8,128)(2,1)} async-done(((bf16[128,160]{0,1:T(8,128)(2,1)}), bf16[128,5120]{0,1:T(8,128)(2,1)}) %all-gather.5.cloned.1.call-update) | async-done | bytes 1310736 | tf_op jit(solution)/shard_map/all_gather | solution.py:51
  323.6 1.8 fusion.21
  325.3 0.4 fusion.5
  325.7 36.5 %all_gather.16 = bf16[128,1536]{0,1:T(8,128)(2,1)S(1)} all-gather(bf16[128,48]{0,1:T(8,128)(2,1)S(1)} %fusion.5), channel_id=1, replica_groups=mesh['expert'=16,'tensor'=32] {'tensor'}, dimensions={1}, use_global_device_ids=true | all-gather | bytes 405504 | tf_op jit(solution)/shard_map/all_gather | solution.py:64
  362.2 0.9 reshape.85
  363.2 1.1 copy-done.5
  364.3 1.1 convolution_bitcast_fusion.1
  366.1 145.7 %all-gather = bf16[512,1,640]{2,1,0:T(2,128)(2,1)S(1)} all-gather(bf16[1,1,640]{2,1,0:T(2,128)(2,1)S(1)} %reshape.76), channel_id=1, replica_groups=mesh['expert'=16,'tensor'=32] {'expert','tensor'}, dimensions={0}, use_global_device_ids=true | all-gather | bytes 656640 | tf_op jit(solution)/shard_map/all_gather | solution.py:78
  511.8 4.0 reduce
  515.8 0.7 reshape.74
  516.7 1.7 reshape.75
  518.4 0.7 exponential_reduce_fusion
  519.1 96.8 %all-reduce = (f32[64]{0:T(128)S(1)}, f32[64]{0:T(128)S(1)}) all-reduce(f32[64]{0:T(128)S(1)} %get-tuple-element.3, f32[64]{0:T(128)S(1)} %get-tuple-element.2), channel_id=1, replica_groups=mesh['expert'=16,'tensor'=32] {'expert','tensor'}, use_global_device_ids=true, to_apply=%region_4.5 | all-reduce | flops 128 | bytes 1024 | tf_op jit(solution)/shard_map/psum | solution.py:89
  615.9 0.5 log_subtract_fusion
  (46 shorter events, 2.1 us)
Async XLA Ops:
  7.2 511.2 %copy-start = (bf16[128,5120]{1,0:T(8,128)(2,1)S(1)}, bf16[128,5120]{1,0:T(8,128)(2,1)}, u32[]{:S(2)}) copy-start(bf16[128,5120]{1,0:T(8,128)(2,1)} %param.20) | copy-start | bytes 3932164
  7.2 145.9 %all-gather.7.cloned.1.call-start = ((), (), s32[]{:S(2)}) async-start(), calls=%async_computation.3 | async-start | bytes 10813440 | tf_op jit(solution)/shard_map/all_gather | solution.py:50
  8.4 3.8 copy-start.10
  12.6 140.5 %copy-start.3 = (bf16[1,48,5120]{2,1,0:T(8,128)(2,1)S(1)}, bf16[1,48,5120]{2,1,0:T(8,128)(2,1)}, u32[]{:S(2)}) copy-start(bf16[1,48,5120]{2,1,0:T(8,128)(2,1)} %param.14) | copy-start | bytes 1474564
  42.6 116.5 %copy-start.4 = (bf16[1,48,5120]{2,1,0:T(8,128)(2,1)S(1)}, bf16[1,48,5120]{2,1,0:T(8,128)(2,1)}, u32[]{:S(2)}) copy-start(bf16[1,48,5120]{2,1,0:T(8,128)(2,1)} %param.15) | copy-start | bytes 1474564
  42.6 199.7 %all-gather.9.cloned.1.call-start = ((), (), s32[]{:S(2)}) async-start(), calls=%async_computation.4 | async-start | bytes 3244032 | tf_op jit(solution)/shard_map/all_gather | solution.py:63
  153.1 7.0 %copy-start.1 = (bf16[1024,5120]{0,1:T(8,128)(2,1)S(1)}, bf16[1024,5120]{0,1:T(8,128)(2,1)}, u32[]{:S(2)}) copy-start(bf16[1024,5120]{0,1:T(8,128)(2,1)} %all-gather.7.cloned.1.call-done) | copy-start | bytes 31457284
  160.0 3.4 copy-start.13
  162.7 160.8 %all-gather.5.cloned.1.call-start = ((), (), s32[]{:S(2)}) async-start(), calls=%async_computation.2 | async-start | bytes 1351680 | tf_op jit(solution)/shard_map/all_gather | solution.py:51
  163.6 78.8 %copy-start.8 = (bf16[1,1536,160]{1,2,0:T(8,128)(2,1)S(1)}, bf16[1,1536,160]{1,2,0:T(8,128)(2,1)}, u32[]{:S(2)}) copy-start(bf16[1,1536,160]{1,2,0:T(8,128)(2,1)} %param.16) | copy-start | bytes 1474564
  250.3 73.2 %copy-start.6 = (bf16[48,5120]{1,0:T(8,128)(2,1)S(1)}, bf16[48,5120]{1,0:T(8,128)(2,1)}, u32[]{:S(2)}) copy-start(bf16[48,5120]{1,0:T(8,128)(2,1)} %param.17) | copy-start | bytes 1474564
  251.8 73.5 %copy-start.7 = (bf16[48,5120]{1,0:T(8,128)(2,1)S(1)}, bf16[48,5120]{1,0:T(8,128)(2,1)}, u32[]{:S(2)}) copy-start(bf16[48,5120]{1,0:T(8,128)(2,1)} %param.18) | copy-start | bytes 1474564
  251.8 110.4 %all-to-all-start.1 = ((bf16[16,2,5120]{2,1,0:T(2,128)(2,1)}), bf16[16,2,5120]{2,1,0:T(2,128)(2,1)S(1)}, u32[]{:S(2)}, u32[]{:S(2)}) async-start(bf16[16,2,5120]{2,1,0:T(2,128)(2,1)} %reshape.84), calls=%async_computation.1 | async-start | bytes 655360 | tf_op jit(solution)/shard_map/all_to_all | solution.py:70
  323.6 1.8 copy-start.2
  363.1 1.2 copy-start.5
  363.1 2.4 copy-start.9
  363.1 2.4 copy-start.11
  365.8 150.0 %copy-start.12 = (bf16[128,160]{0,1:T(8,128)(2,1)}, bf16[128,160]{0,1:T(8,128)(2,1)S(1)}, u32[]{:S(2)}) copy-start(bf16[128,160]{0,1:T(8,128)(2,1)S(1)} %fusion.4) | copy-start | bytes 122884
  516.7 1.7 copy-start.14
Sparse Core Ops, SparseCore 0:
  42.7 110.3 all-gather.6
  162.8 79.4 all-gather.8
  245.5 78.0 all-gather.4
where the time goes:
time: 623 us
  blocking collectives  308 us (49%)
  waiting for transfers between devices  247 us (40%)
  matrix products  19.8 us (3%)
  between operations  14.1 us (2%)
  starting transfers between devices  12.1 us (2%)
  other arithmetic  11.4 us (2%)
  local copies, waits for them, and re-layouts  10.7 us (2%)
    all_gather x1, blocking collectives, shards(): collected = lax.all_gather(scored, ('expert', 'tensor'), axis=0, tiled=True)  146 us
    all_gather x1, waiting for transfers between devices, shards(): lax.all_gather(flat_rows, 'tensor', axis=1, tiled=True)  110 us
    psum x1, blocking collectives, shards(): lax.psum((exp_sums, target_part), ('expert', 'tensor'))  96.8 us
    all_gather x1, waiting for transfers between devices, shards(): lax.all_gather(flat_hidden, 'tensor', axis=1, tiled=True)  76 us
    all_gather x1, waiting for transfers between devices, shards(): lax.all_gather(tokens, 'tensor', axis=1, tiled=True)  60 us
    all_gather x1, blocking collectives, shards(): lax.all_gather(hidden_shared, 'tensor', axis=1, tiled=True)  36.5 us
    all_to_all x1, blocking collectives, shards(): lax.all_to_all(outgoing, 'expert', split_axis=0, concat_axis=1, tiled=True)  29.1 us
  transfers between devices with their start and end apart: 4, of which 3 were waited for; matrix products, arithmetic and copies ran while one was open for 2% of the time, Pallas kernels for 0%

commit v1 on v0

--- a/solution.py
+++ b/solution.py
@@ -5,6 +5,14 @@
 
 EXPERTS = 16
 SCORE_E = 4
+
+
+def tiled_gather(array, axis, dim):
+    size = lax.axis_size(axis)
+    repeats = [size if d == dim else 1 for d in range(array.ndim)]
+    return lax.all_to_all(
+        jnp.tile(array, repeats), axis, split_axis=dim, concat_axis=dim, tiled=True
+    )
 
 
 def slot_tables(routes, gates, capacity):
@@ -61,7 +69,7 @@
     flat_hidden = hidden_routed.reshape(exp_dev * slot_count, width)
     pieces = (
         lax.all_gather(flat_hidden, "tensor", axis=1, tiled=True),
-        lax.all_gather(hidden_shared, "tensor", axis=1, tiled=True),
+        tiled_gather(hidden_shared, "tensor", 1),
     )
     span = pieces[0].shape[1]
     rows = pieces[0].reshape(exp_dev, slot_count, span)

time: 623 us -> 591 us (0.949)
  blocking collectives: 308 us -> 262 us
  waiting for transfers between devices: 247 us -> 254 us
    all_gather x1 -> x0, blocking collectives: 36.5 us -> none  [shards(): lax.all_gather(hidden_shared, 'tensor', axis=1, tiled=True)]
    all_gather x1, blocking collectives: 146 us -> 136 us  [shards(): collected = lax.all_gather(scored, ('expert', 'tensor'), axis=0, tiled=True)]
  transfers between devices with their start and end apart: 4 -> 5, of which waited for: 3 -> 4; matrix products, arithmetic and copies ran while one was open for 2% -> 3% of each run, Pallas kernels for 0% -> 0%
where the time goes in v1:
time: 591 us; the launch traced here: 590 us
  blocking collectives  262 us (44%)
  waiting for transfers between devices  254 us (43%)
  matrix products  19.8 us (3%)
  starting transfers between devices  18 us (3%)
  between operations  14.1 us (2%)
  local copies, waits for them, and re-layouts  11.5 us (2%)
  other arithmetic  11.4 us (2%)
    all_gather x1, blocking collectives, shards(): collected = lax.all_gather(scored, ('expert', 'tensor'), axis=0, tiled=True)  136 us
    all_gather x1, waiting for transfers between devices, shards(): lax.all_gather(flat_rows, 'tensor', axis=1, tiled=True)  110 us
    psum x1, blocking collectives, shards(): lax.psum((exp_sums, target_part), ('expert', 'tensor'))  96.8 us
    all_gather x1, waiting for transfers between devices, shards(): lax.all_gather(flat_hidden, 'tensor', axis=1, tiled=True)  78.9 us
    all_gather x1, waiting for transfers between devices, shards(): lax.all_gather(tokens, 'tensor', axis=1, tiled=True)  59.9 us
    all_to_all x1, blocking collectives, shards(): lax.all_to_all(outgoing, 'expert', split_axis=0, concat_axis=1, tiled=True)  29.1 us
  transfers between devices with their start and end apart: 5, of which 4 were waited for; matrix products, arithmetic and copies ran while one was open for 3% of the time, Pallas kernels for 0%

profile of v1, /device:TPU:1, one launch (start us, length us, event | category | flops | bytes accessed | tf_op | source)
XLA Modules:
  0.0 590.4 jit_solution(9935480038216036610)
XLA Ops:
  7.2 0.9 copy.22
  8.6 2.4 select_reduce_fusion
  11.0 1.2 fusion
  12.6 29.1 %all_to_all.30 = bf16[16,64,160]{2,1,0:T(8,128)(2,1)S(1)} all-to-all(bf16[16,64,160]{2,1,0:T(8,128)(2,1)S(1)} %convolution_convert_fusion.1), channel_id=1, replica_groups=mesh['expert'=16,'tensor'=32] {'expert'}, dimensions={0} | all-to-all | bytes 655360 | tf_op jit(solution)/shard_map/all_to_all | solution.py:54
  41.7 0.9 copy.25
  42.7 110.4 %all-gather.7.cloned.1.call-done = bf16[1024,5120]{0,1:T(8,128)(2,1)} async-done(((bf16[1024,160]{0,1:T(8,128)(2,1)}), bf16[1024,5120]{0,1:T(8,128)(2,1)}) %all-gather.7.cloned.1.call-update) | async-done | bytes 10485776 | tf_op jit(solution)/shard_map/all_gather | solution.py:58
  153.1 6.1 %fusion.11 = f32[1024,48]{0,1:T(8,128)S(1)} fusion(bf16[1024,5120]{0,1:T(8,128)(2,1)} %all-gather.7.cloned.1.call-done, bf16[1,48,5120]{2,1,0:T(8,128)(2,1)S(1)} %copy-done.3), kind=kOutput, calls=%fused_computation.24 | convolution fusion | flops 503316480 | bytes 11173888 | tf_op jit(solution)/shard_map/erw,efw->erf/dot_general | solution.py:63
  159.2 0.9 copy-done.1
  160.0 2.6 fusion.2
  163.4 78.9 %all-gather.9.cloned.1.call-done = bf16[1024,1536]{0,1:T(8,128)(2,1)} async-done(((bf16[1024,48]{0,1:T(8,128)(2,1)}), bf16[1024,1536]{0,1:T(8,128)(2,1)}) %all-gather.9.cloned.1.call-update) | async-done | bytes 3145744 | tf_op jit(solution)/shard_map/all_gather | solution.py:71
  242.3 2.6 fusion.1
  244.9 0.8 copy.26
  245.8 0.5 broadcast.31
  246.3 4.0 reduce.1
  250.3 1.5 reshape.91
  251.9 11.8 %all-to-all-start.2 = ((bf16[16,2,5120]{2,1,0:T(2,128)(2,1)}), bf16[16,2,5120]{2,1,0:T(2,128)(2,1)S(1)}, u32[]{:S(2)}, u32[]{:S(2)}) async-start(bf16[16,2,5120]{2,1,0:T(2,128)(2,1)} %reshape.91), calls=%async_computation.2 | async-start | bytes 655360 | tf_op jit(solution)/shard_map/all_to_all | solution.py:78
  263.6 59.9 %all-gather.5.cloned.1.call-done = bf16[128,5120]{0,1:T(8,128)(2,1)} async-done(((bf16[128,160]{0,1:T(8,128)(2,1)}), bf16[128,5120]{0,1:T(8,128)(2,1)}) %all-gather.5.cloned.1.call-update) | async-done | bytes 1310736 | tf_op jit(solution)/shard_map/all_gather | solution.py:59
  323.6 1.8 fusion.21
  325.7 0.8 tile.2
  326.5 5.9 %all-to-all-start = ((bf16[128,32,48]{0,2,1:T(8,128)(2,1)}), bf16[128,32,48]{0,2,1:T(8,128)(2,1)S(1)}, u32[]{:S(2)}, u32[]{:S(2)}) async-start(bf16[128,32,48]{0,2,1:T(8,128)(2,1)} %tile.2), calls=%async_computation | async-start | bytes 786432 | tf_op jit(solution)/shard_map/all_to_all | solution.py:13
  332.6 2.7 convolution_bitcast_fusion
  335.3 0.9 reshape.92
  336.4 1.1 copy-done.5
  337.5 1.1 convolution_bitcast_fusion.1
  338.6 4.1 all-to-all-done
  343.3 135.9 %all-gather = bf16[512,1,640]{2,1,0:T(2,128)(2,1)S(1)} all-gather(bf16[1,1,640]{2,1,0:T(2,128)(2,1)S(1)} %reshape.83), channel_id=1, replica_groups=mesh['expert'=16,'tensor'=32] {'expert','tensor'}, dimensions={0}, use_global_device_ids=true | all-gather | bytes 656640 | tf_op jit(solution)/shard_map/all_gather | solution.py:86
  479.2 4.0 reduce
  483.2 0.7 reshape.81
  484.1 1.7 reshape.82
  485.8 0.7 exponential_reduce_fusion
  486.5 96.8 %all-reduce = (f32[64]{0:T(128)S(1)}, f32[64]{0:T(128)S(1)}) all-reduce(f32[64]{0:T(128)S(1)} %get-tuple-element.3, f32[64]{0:T(128)S(1)} %get-tuple-element.2), channel_id=1, replica_groups=mesh['expert'=16,'tensor'=32] {'expert','tensor'}, use_global_device_ids=true, to_apply=%region_4.5 | all-reduce | flops 128 | bytes 1024 | tf_op jit(solution)/shard_map/psum | solution.py:97
  583.4 0.5 log_subtract_fusion
  (48 shorter events, 3.0 us)
Async XLA Ops:
  7.2 478.7 %copy-start = (bf16[128,5120]{1,0:T(8,128)(2,1)S(1)}, bf16[128,5120]{1,0:T(8,128)(2,1)}, u32[]{:S(2)}) copy-start(bf16[128,5120]{1,0:T(8,128)(2,1)} %param.20) | copy-start | bytes 3932164
  7.2 145.9 %all-gather.7.cloned.1.call-start = ((), (), s32[]{:S(2)}) async-start(), calls=%async_computation.4 | async-start | bytes 10813440 | tf_op jit(solution)/shard_map/all_gather | solution.py:58
  8.4 3.8 copy-start.10
  12.6 140.5 %copy-start.3 = (bf16[1,48,5120]{2,1,0:T(8,128)(2,1)S(1)}, bf16[1,48,5120]{2,1,0:T(8,128)(2,1)}, u32[]{:S(2)}) copy-start(bf16[1,48,5120]{2,1,0:T(8,128)(2,1)} %param.14) | copy-start | bytes 1474564
  42.6 116.5 %copy-start.4 = (bf16[1,48,5120]{2,1,0:T(8,128)(2,1)S(1)}, bf16[1,48,5120]{2,1,0:T(8,128)(2,1)}, u32[]{:S(2)}) copy-start(bf16[1,48,5120]{2,1,0:T(8,128)(2,1)} %param.15) | copy-start | bytes 1474564
  42.6 199.7 %all-gather.9.cloned.1.call-start = ((), (), s32[]{:S(2)}) async-start(), calls=%async_computation.5 | async-start | bytes 3244032 | tf_op jit(solution)/shard_map/all_gather | solution.py:71
  153.1 7.0 %copy-start.1 = (bf16[1024,5120]{0,1:T(8,128)(2,1)S(1)}, bf16[1024,5120]{0,1:T(8,128)(2,1)}, u32[]{:S(2)}) copy-start(bf16[1024,5120]{0,1:T(8,128)(2,1)} %all-gather.7.cloned.1.call-done) | copy-start | bytes 31457284
  160.0 82.3 %copy-start.8 = (bf16[1,1536,160]{1,2,0:T(8,128)(2,1)S(1)}, bf16[1,1536,160]{1,2,0:T(8,128)(2,1)}, u32[]{:S(2)}) copy-start(bf16[1,1536,160]{1,2,0:T(8,128)(2,1)} %param.16) | copy-start | bytes 1474564
  162.7 160.9 %all-gather.5.cloned.1.call-start = ((), (), s32[]{:S(2)}) async-start(), calls=%async_computation.3 | async-start | bytes 1351680 | tf_op jit(solution)/shard_map/all_gather | solution.py:59
  250.3 73.2 %copy-start.6 = (bf16[48,5120]{1,0:T(8,128)(2,1)S(1)}, bf16[48,5120]{1,0:T(8,128)(2,1)}, u32[]{:S(2)}) copy-start(bf16[48,5120]{1,0:T(8,128)(2,1)} %param.17) | copy-start | bytes 1474564
  251.9 73.5 %copy-start.7 = (bf16[48,5120]{1,0:T(8,128)(2,1)S(1)}, bf16[48,5120]{1,0:T(8,128)(2,1)}, u32[]{:S(2)}) copy-start(bf16[48,5120]{1,0:T(8,128)(2,1)} %param.18) | copy-start | bytes 1474564
  251.9 73.9 %all-to-all-start.2 = ((bf16[16,2,5120]{2,1,0:T(2,128)(2,1)}), bf16[16,2,5120]{2,1,0:T(2,128)(2,1)S(1)}, u32[]{:S(2)}, u32[]{:S(2)}) async-start(bf16[16,2,5120]{2,1,0:T(2,128)(2,1)} %reshape.91), calls=%async_computation.2 | async-start | bytes 655360 | tf_op jit(solution)/shard_map/all_to_all | solution.py:78
  323.6 1.8 copy-start.2
  325.3 7.1 %copy-start.13 = (f32[128,6]{0,1:T(8,128)S(1)}, f32[128,6]{0,1:T(8,128)}, u32[]{:S(2)}) copy-start(f32[128,6]{0,1:T(8,128)} %param.13) | copy-start | bytes 9220
  326.5 16.2 %all-to-all-start = ((bf16[128,32,48]{0,2,1:T(8,128)(2,1)}), bf16[128,32,48]{0,2,1:T(8,128)(2,1)S(1)}, u32[]{:S(2)}, u32[]{:S(2)}) async-start(bf16[128,32,48]{0,2,1:T(8,128)(2,1)} %tile.2), calls=%async_computation | async-start | bytes 786432 | tf_op jit(solution)/shard_map/all_to_all | solution.py:13
  336.2 1.2 copy-start.5
  336.2 6.5 %copy-start.9 = (bf16[1536,160]{0,1:T(8,128)(2,1)S(1)}, bf16[1536,160]{0,1:T(8,128)(2,1)}, u32[]{:S(2)}) copy-start(bf16[1536,160]{0,1:T(8,128)(2,1)} %param.19) | copy-start | bytes 1474564
  336.3 6.4 %copy-start.11 = (bf16[128,160]{0,1:T(8,128)(2,1)S(1)}, bf16[128,160]{0,1:T(8,128)(2,1)}, u32[]{:S(2)}) copy-start(bf16[128,160]{0,1:T(8,128)(2,1)} %param.11) | copy-start | bytes 122884
  343.0 140.2 %copy-start.12 = (bf16[128,160]{0,1:T(8,128)(2,1)}, bf16[128,160]{0,1:T(8,128)(2,1)S(1)}, u32[]{:S(2)}) copy-start(bf16[128,160]{0,1:T(8,128)(2,1)S(1)} %fusion.4) | copy-start | bytes 122884
  484.1 1.7 copy-start.14
Sparse Core Ops, SparseCore 0:
  42.7 110.3 all-gather.6
  162.8 79.4 all-gather.8
  245.5 78.0 all-gather.4
